TPU v7x, 32 devices: a whole 2x2x4 slice. The times are simulated.
32 devices in a mesh: dp: 4 (over z), vocab: 8 (over y, x, core).
Axes of the slice: x: 2, y: 2, z: 4, core: 2. Of those that a mesh axis runs over, the one named last changes fastest.
Arguments:
- packed_symbol_codes: int32 [32, 1024], P(('dp', 'vocab')), may hold values from 0 to 50256
- article_numbering: int32 [32, 1024], P(('dp', 'vocab')), may hold values from 0 to 19, never falling along the last dimension, each value on 1 to 256 neighbouring positions
- target_spots: int32 [32, 128], P(('dp', 'vocab')), may hold values from 0 to 1022
- answer_flags: int32 [32, 128], P(('dp', 'vocab')), may hold values 0 or 1
- shared_embedding: bfloat16 [50304, 1024], P('vocab'), may hold values from -0.6 to 0.6
- spot_embedding: bfloat16 [1024, 1024], replicated, may hold values from -0.359375 to 0.359375
- combined_qkv_weights: bfloat16 [1024, 3072], replicated, may hold values from -0.1875 to 0.1875
- attend_outgoing_weights: bfloat16 [1024, 1024], replicated, may hold values from -0.5 to 0.5
- dense_incoming_weights: bfloat16 [1024, 4096], replicated, may hold values from -0.1875 to 0.1875
- dense_outgoing_weights: bfloat16 [4096, 1024], replicated, may hold values from -0.09375 to 0.09375
- layernorm_affine: float32 [6, 1024], replicated, may hold values from -0.6 to 1.3, as said below
- bias_terms: float32 [9216], replicated, may hold values from -1.2 to 1.2
- adaptor_float_copies: float32 [73728], replicated, may hold values from -0.09375 to 0.09375
- average_moments: float32 [73728], replicated, may hold values from -1.2276159e-07 to 1.2276159e-07
- squared_moments: float32 [73728], replicated, may hold values from 1.3576945e-16 to 5.430778e-16
Outputs:
- refreshed_thin_pairs: float32 [73728], replicated
- updated_first_moment: float32 [73728], replicated
- updated_second_moment: float32 [73728], replicated
- gradient_global_norm: float32 [], replicated
- smoothed_entropy_cost: float32 [], replicated
Inputs may be any that keep to these rules, and one draw needn't show every extreme that they name: `article_numbering`: within a slot the document numbers never fall, every document has 1 to 256 tokens. `layernorm_affine`: rows 0 to 2 are gains, rows 3 to 5 shifts.
All inputs are finite; a program needn't handle non-finite values. No bound on the sum of `answer_flags` on one device may be relied on, other than what follows from the above.
Results may differ from a plain program's by a relative error of at most 0.00085.
The roundings to bfloat16 on the way count: a program that leaves them out, or rounds other values in their place, can miss the bound.
Values may be sent and summed in bfloat16 or wider, within the bound.
A program may use at most 320 MiB of HBM per device.

v0:
```python
from functools import partial
import math
import jax
import jax.numpy as jnp
from jax import lax
from jax.sharding import PartitionSpec as P

MODEL_WIDTH = 1024
HEADS = 16
FEEDFWD_UNITS = 4096
VOCAB_SIZE = 50257
RANK = 4
STEP = 10
ADAPTER_SCALE = 8.0
NORM_EPS = 1e-05
GRAD_CLIP = 0.0001
STRIDE_LENGTH = 0.02
BETA_ONE = 0.9
BETA_TWO = 0.999
SHRINK_PENALTY = 0.01
STABILITY_FLOOR = 1e-08
MASKED = -1e30


def matrix_multiply(left, right):
    return jnp.dot(left, right, preferred_element_type=jnp.float32)


def matrix_multiply_transposed_left(left, right):
    return lax.dot_general(
        left, right, (((0,), (0,)), ((), ())), preferred_element_type=jnp.float32
    )


def matrix_multiply_transposed_right(left, right):
    return lax.dot_general(
        left, right, (((1,), (1,)), ((), ())), preferred_element_type=jnp.float32
    )


def layer_norm(stream, gain, shift):
    centred = stream - jnp.mean(stream, axis=-1, keepdims=True)
    spread = lax.rsqrt(jnp.mean(centred * centred, axis=-1, keepdims=True) + NORM_EPS)
    return centred * spread * gain + shift


def positions(segments):
    steps_here = jnp.arange(segments.shape[0], dtype=jnp.int32)
    earlier = (segments[None, :] == segments[:, None]) & (steps_here[None, :] < steps_here[:, None])
    return jnp.sum(earlier.astype(jnp.int32), axis=1)


def distinct_thin_pairs(stacked_samples):
    shapes = [
        (MODEL_WIDTH, 3 * RANK),
        (3, RANK, MODEL_WIDTH),
        (MODEL_WIDTH, RANK),
        (RANK, MODEL_WIDTH),
        (MODEL_WIDTH, RANK),
        (RANK, FEEDFWD_UNITS),
        (FEEDFWD_UNITS, RANK),
        (RANK, MODEL_WIDTH),
    ]
    pieces = []
    offset = 0
    for shape in shapes:
        number = math.prod(shape)
        pieces.append(stacked_samples[offset : offset + number].reshape(shape))
        offset += number
    return pieces


def block_diagonal_mask(blocks):
    number, rank, width = blocks.shape
    eye = jnp.eye(number, dtype=blocks.dtype)
    return (eye[:, None, :, None] * blocks[:, :, None, :]).reshape(number * rank, number * width)


def select_rows(onehot, rows):
    return matrix_multiply(onehot, rows).astype(jnp.bfloat16)


def split_heads(rows):
    return rows.reshape(rows.shape[0], HEADS, rows.shape[1] // HEADS)


def logit_grads(masked_logits, log_total, hit, active_positions, row_weight, denom):
    grad_logits = (row_weight / denom)[:, None] * (
        jnp.exp(masked_logits - log_total[:, None])
        - 0.9 * hit.astype(jnp.float32)
        - 0.1 / VOCAB_SIZE * active_positions.astype(jnp.float32)[None, :]
    )
    return grad_logits.astype(jnp.bfloat16)


def adaptive_moment_update(grad, weight, first, second):
    first_new = BETA_ONE * first + (1.0 - BETA_ONE) * grad
    second_new = BETA_TWO * second + (1.0 - BETA_TWO) * grad * grad
    debiased_mean_estimate = first_new / (1.0 - BETA_ONE**STEP)
    debiased_variance_estimate = second_new / (1.0 - BETA_TWO**STEP)
    weight_new = weight - STRIDE_LENGTH * (
        debiased_mean_estimate / (jnp.sqrt(debiased_variance_estimate) + STABILITY_FLOOR)
        + SHRINK_PENALTY * weight
    )
    return (weight_new, first_new, second_new)


def local(
    packed_symbol_codes,
    article_numbering,
    target_spots,
    answer_flags,
    shared_embedding,
    spot_embedding,
    combined_qkv_weights,
    attend_outgoing_weights,
    dense_incoming_weights,
    dense_outgoing_weights,
    layernorm_affine,
    bias_terms,
    adaptor_float_copies,
    average_moments,
    squared_moments,
):
    tokens_here = packed_symbol_codes[0]
    segments = article_numbering[0]
    spot_objective = target_spots[0]
    rows_here = spot_objective.shape[0]
    shard_rows = shared_embedding.shape[0]
    table_base = lax.axis_index("vocab") * shard_rows
    all_tokens = lax.all_gather(packed_symbol_codes, "vocab", axis=0, tiled=True).reshape(-1)
    wanted = all_tokens - table_base
    inside = (wanted >= 0) & (wanted < shard_rows)
    picked = jnp.take(shared_embedding, jnp.clip(wanted, 0, shard_rows - 1), axis=0)
    embedded = lax.psum_scatter(
        jnp.where(inside[:, None], picked.astype(jnp.float32), 0.0).astype(jnp.bfloat16),
        "vocab",
        scatter_dimension=0,
        tiled=True,
    ).astype(jnp.float32)
    stream = embedded + jnp.take(spot_embedding, positions(segments), axis=0).astype(jnp.float32)
    a_qkv, b_qkv, a_o, b_o, a_fc, b_fc, a_p, b_p = [
        lexicon_portion.astype(jnp.bfloat16)
        for lexicon_portion in distinct_thin_pairs(adaptor_float_copies)
    ]
    width = stream.shape[1]
    hidden_width = dense_incoming_weights.shape[1]
    length = stream.shape[0]
    onehot = spot_objective[:, None] == jnp.arange(length, dtype=jnp.int32)[None, :]
    pick = onehot.astype(jnp.bfloat16)
    h1 = layer_norm(stream, layernorm_affine[0], layernorm_affine[3]).astype(jnp.bfloat16)
    stream_rows = jnp.take(stream, spot_objective, axis=0)
    h1_rows = select_rows(pick, h1)
    u1 = matrix_multiply(h1, a_qkv).astype(jnp.bfloat16)
    u1_rows = select_rows(pick, u1)
    q = (
        matrix_multiply(h1_rows, combined_qkv_weights[:, :width])
        + bias_terms[:width]
        + ADAPTER_SCALE * matrix_multiply(u1_rows[:, :RANK], b_qkv[0])
    ).astype(jnp.bfloat16)
    kv = (
        matrix_multiply(h1, combined_qkv_weights[:, width:])
        + bias_terms[width : 3 * width]
        + ADAPTER_SCALE * matrix_multiply(u1[:, RANK:], block_diagonal_mask(b_qkv[1:]))
    ).astype(jnp.bfloat16)
    queries, keys_all, values_all = (
        split_heads(q),
        split_heads(kv[:, :width]),
        split_heads(kv[:, width:]),
    )
    scale = queries.shape[2] ** (-0.5)
    there = jnp.arange(length, dtype=jnp.int32)[None, :]
    segment_rows = jnp.take(segments, spot_objective)
    allowed = (there <= spot_objective[:, None]) & (segment_rows[:, None] == segments[None, :])
    scores = (
        jnp.einsum("qhd,khd->hqk", queries, keys_all, preferred_element_type=jnp.float32) * scale
    )
    scores = jnp.where(allowed[None], scores, MASKED)
    top = jnp.max(scores, axis=2, keepdims=True)
    expd = jnp.exp(scores - top)
    probs = expd / jnp.sum(expd, axis=2, keepdims=True)
    probs_low = probs.astype(jnp.bfloat16)
    o = (
        jnp.einsum("hqk,khd->qhd", probs_low, values_all, preferred_element_type=jnp.float32)
        .reshape(rows_here, width)
        .astype(jnp.bfloat16)
    )
    uo = matrix_multiply(o, a_o).astype(jnp.bfloat16)
    middle = (
        stream_rows
        + matrix_multiply(o, attend_outgoing_weights)
        + bias_terms[3 * width : 4 * width]
        + ADAPTER_SCALE * matrix_multiply(uo, b_o)
    )
    h2, norm_two_back = jax.vjp(
        lambda value: layer_norm(value, layernorm_affine[1], layernorm_affine[4]), middle
    )
    h2 = h2.astype(jnp.bfloat16)
    uf = matrix_multiply(h2, a_fc).astype(jnp.bfloat16)
    pre = (
        matrix_multiply(h2, dense_incoming_weights)
        + bias_terms[4 * width : 4 * width + hidden_width]
        + ADAPTER_SCALE * matrix_multiply(uf, b_fc)
    )
    f, gelu_back = jax.vjp(partial(jax.nn.gelu, approximate=True), pre)
    f = f.astype(jnp.bfloat16)
    up = matrix_multiply(f, a_p).astype(jnp.bfloat16)
    output = (
        middle
        + matrix_multiply(f, dense_outgoing_weights)
        + bias_terms[4 * width + hidden_width :]
        + ADAPTER_SCALE * matrix_multiply(up, b_p)
    )
    closing_result, final_back = jax.vjp(
        lambda value: layer_norm(value, layernorm_affine[2], layernorm_affine[5]), output
    )
    final_rows = closing_result.astype(jnp.bfloat16)
    next_places = spot_objective + 1
    targets = jnp.take(tokens_here, next_places)
    weights_here = answer_flags[0] * (
        jnp.take(segments, spot_objective) == jnp.take(segments, next_places)
    ).astype(jnp.int32)
    all_labels = lax.all_gather(
        jnp.stack([targets, weights_here], axis=1), "vocab", axis=0, tiled=True
    )
    class_scores = matrix_multiply_transposed_right(
        lax.all_gather(final_rows, "vocab", axis=0, tiled=True), shared_embedding
    )
    vocab_ids = table_base + jnp.arange(shard_rows, dtype=jnp.int32)
    active_positions = vocab_ids < VOCAB_SIZE
    masked_logits = jnp.where(active_positions[None, :], class_scores, -jnp.inf)
    local_top = jnp.max(masked_logits, axis=1)
    smooth_local = jnp.sum(jnp.where(active_positions[None, :], class_scores, 0.0), axis=1)
    hit = vocab_ids[None, :] == all_labels[:, 0:1]
    target_local = jnp.sum(jnp.where(hit, class_scores, 0.0), axis=1)
    top = lax.pmax(local_top, "vocab")
    local_sum = jnp.sum(jnp.exp(masked_logits - top[:, None]), axis=1)
    exp_sum, smooth_sum, target_logit = lax.psum((local_sum, smooth_local, target_local), "vocab")
    log_total = top + jnp.log(exp_sum)
    row_weight = all_labels[:, 1].astype(jnp.float32)
    row_loss = log_total - 0.9 * target_logit - 0.1 * smooth_sum / VOCAB_SIZE
    loss_sum, weight_sum = lax.psum((jnp.sum(row_weight * row_loss), jnp.sum(row_weight)), "dp")
    denom = jnp.maximum(weight_sum, 1.0)
    smoothed_entropy_cost = loss_sum / denom
    grad_logits = logit_grads(masked_logits, log_total, hit, active_positions, row_weight, denom)
    grad_rows = lax.psum_scatter(
        matrix_multiply(
            lax.slice_in_dim(grad_logits, 0, rows_here * lax.axis_size("vocab"), axis=0),
            shared_embedding,
        ),
        "vocab",
        scatter_dimension=0,
        tiled=True,
    )
    same = spot_objective[:, None] == spot_objective[None, :]
    order = jnp.arange(rows_here, dtype=jnp.int32)
    repeat = jnp.any(same & (order[None, :] < order[:, None]), axis=1)
    merge = (same & ~repeat[:, None]).astype(jnp.float32)
    grad_final = jnp.dot(merge, grad_rows, precision=lax.Precision.HIGHEST)
    (dx3,) = final_back(grad_final)
    dm = dx3.astype(jnp.bfloat16)
    g_bp = ADAPTER_SCALE * matrix_multiply_transposed_left(up, dm)
    du_p = (ADAPTER_SCALE * matrix_multiply_transposed_right(dm, b_p)).astype(jnp.bfloat16)
    g_ap = matrix_multiply_transposed_left(f, du_p)
    df = matrix_multiply_transposed_right(
        dm, dense_outgoing_weights
    ) + matrix_multiply_transposed_right(du_p, a_p)
    (dpre,) = gelu_back(df)
    dpre = dpre.astype(jnp.bfloat16)
    g_bfc = ADAPTER_SCALE * matrix_multiply_transposed_left(uf, dpre)
    du_f = (ADAPTER_SCALE * matrix_multiply_transposed_right(dpre, b_fc)).astype(jnp.bfloat16)
    g_afc = matrix_multiply_transposed_left(h2, du_f)
    dh2 = matrix_multiply_transposed_right(
        dpre, dense_incoming_weights
    ) + matrix_multiply_transposed_right(du_f, a_fc)
    (grad_middle,) = norm_two_back(dh2)
    dx2 = dx3 + grad_middle
    da = dx2.astype(jnp.bfloat16)
    g_bo = ADAPTER_SCALE * matrix_multiply_transposed_left(uo, da)
    du_o = (ADAPTER_SCALE * matrix_multiply_transposed_right(da, b_o)).astype(jnp.bfloat16)
    g_ao = matrix_multiply_transposed_left(o, du_o)
    do = (
        matrix_multiply_transposed_right(da, attend_outgoing_weights)
        + matrix_multiply_transposed_right(du_o, a_o)
    ).astype(jnp.bfloat16)
    do = split_heads(do)
    dv = jnp.einsum("hqk,qhd->khd", probs_low, do, preferred_element_type=jnp.float32)
    dp = jnp.einsum("qhd,khd->hqk", do, values_all, preferred_element_type=jnp.float32)
    ds = (probs * (dp - jnp.sum(probs * dp, axis=2, keepdims=True))).astype(jnp.bfloat16)
    dq = jnp.einsum("hqk,khd->qhd", ds, keys_all, preferred_element_type=jnp.float32) * scale
    dk = jnp.einsum("hqk,qhd->khd", ds, queries, preferred_element_type=jnp.float32) * scale
    dq = dq.reshape(rows_here, width).astype(jnp.bfloat16)
    dk = dk.reshape(length, width).astype(jnp.bfloat16)
    dv = dv.reshape(length, width).astype(jnp.bfloat16)
    thirds = ((h1_rows, u1_rows, dq), (h1, u1, dk), (h1, u1, dv))
    g_bqkv = []
    g_aqkv = []
    for j, (normed, low, grad) in enumerate(thirds):
        low = low[:, j * RANK : (j + 1) * RANK]
        g_bqkv.append(ADAPTER_SCALE * matrix_multiply_transposed_left(low, grad))
        du = (ADAPTER_SCALE * matrix_multiply_transposed_right(grad, b_qkv[j])).astype(jnp.bfloat16)
        g_aqkv.append(matrix_multiply_transposed_left(normed, du))
    pieces = [
        jnp.concatenate(g_aqkv, axis=1),
        jnp.concatenate(g_bqkv, axis=0),
        g_ao,
        g_bo,
        g_afc,
        g_bfc,
        g_ap,
        g_bp,
    ]
    local_grad = jnp.concatenate([piece.reshape(-1) for piece in pieces])
    grad_total = lax.psum(local_grad, ("dp", "vocab"))
    gradient_global_norm = jnp.sqrt(jnp.sum(grad_total * grad_total))
    capped_derivative = grad_total * (GRAD_CLIP / jnp.maximum(gradient_global_norm, GRAD_CLIP))
    refreshed_thin_pairs, updated_first_moment, updated_second_moment = adaptive_moment_update(
        capped_derivative, adaptor_float_copies, average_moments, squared_moments
    )
    return (
        refreshed_thin_pairs,
        updated_first_moment,
        updated_second_moment,
        gradient_global_norm,
        smoothed_entropy_cost,
    )


def solution(mesh):
    return jax.shard_map(
        local,
        mesh=mesh,
        in_specs=(
            P(("dp", "vocab"), None),
            P(("dp", "vocab"), None),
            P(("dp", "vocab"), None),
            P(("dp", "vocab"), None),
            P("vocab", None),
            P(),
            P(),
            P(),
            P(),
            P(),
            P(),
            P(),
            P(),
            P(),
            P(),
        ),
        out_specs=(P(), P(), P(), P(), P()),
        check_vma=False,
    )
```

profile of v0, /device:TPU:8, one launch (start us, length us, event | category | flops | bytes accessed | tf_op | source)
XLA Modules:
  0.0 644.7 jit_solution(2936452298662439854)
XLA Ops:
  7.2 9.4 %all-gather = s32[8,1,1024]{2,1,0:T(1,128)S(1)} all-gather(s32[1,1,1024]{2,1,0:T(1,128)} %bitcast.159), channel_id=1, replica_groups=mesh['dp'=4,'vocab'=8] {'vocab'}, dimensions={0}, use_global_device_ids=true | all-gather | bytes 36864 | tf_op jit(solution)/shard_map/all_gather | solution.py:131
  16.9 47.0 %gather_fusion = bf16[8192,1024]{1,0:T(8,128)(2,1)} fusion(bf16[6288,1024]{1,0:T(8,128)(2,1)} %param.21, s32[8192]{0:T(1024)S(1)} %broadcast_clamp_fusion), kind=kCustom, calls=%fused_computation.3 | custom fusion | bytes 33587200 | tf_op jit(solution)/shard_map/jit(_take)/gather | solution.py:134
  63.9 15.2 %select_convert_fusion = bf16[8192,1024]{1,0:T(8,128)(2,1)} fusion(bf16[8192,1024]{1,0:T(8,128)(2,1)} %gather_fusion, pred[8192]{0:T(1024)(128)(4,1)S(1)} %compare_and_fusion.3, pred[8192]{0:T(1024)(128)(4,1)S(1)} %bitcast.197), kind=kLoop, calls=%fused_computation.7 | loop fusion | flops 33554432 | bytes 33570816 | tf_op jit(solution)/shard_map/convert_element_type | solution.py:136
  90.2 5.4 gather_fusion.1
  98.8 96.5 %reduce-scatter.3.cloned.1.call-done = bf16[1024,1024]{1,0:T(8,128)(2,1)} async-done(((bf16[8192,1024]{1,0:T(8,128)(2,1)}), bf16[1024,1024]{1,0:T(8,128)(2,1)}) %reduce-scatter.3.cloned.1.call-update) | async-done | bytes 2097168 | tf_op jit(solution)/shard_map/reduce_scatter | solution.py:135
  203.9 6.8 %fusion.12 = f32[1024,2048]{1,0:T(8,128)} fusion(bf16[1024,1024]{1,0:T(8,128)(2,1)S(1)} %add_convert_fusion.1, bf16[1024,3072]{1,0:T(8,128)(2,1)S(1)} %bitcast.214), kind=kOutput, calls=%fused_computation.34 | convolution fusion | flops 4294967296 | bytes 14680064 | tf_op jit(solution)/shard_map/dot_general | solution.py:26
  211.6 4.8 add_convert_fusion
  221.8 4.8 copy.46
  226.5 4.2 gather_fusion.2
  230.7 6.3 fusion.98
  237.6 6.1 fusion.44
  252.9 8.8 %all_gather.10 = s32[1024,2]{0,1:T(2,128)S(1)} all-gather(s32[128,2]{0,1:T(2,128)S(1)} %pad_add_fusion), channel_id=1, replica_groups=mesh['dp'=4,'vocab'=8] {'vocab'}, dimensions={0}, use_global_device_ids=true | all-gather | bytes 9216 | tf_op jit(solution)/shard_map/all_gather | solution.py:223
  263.0 17.9 %all-gather.3.cloned.1.call-done = bf16[1024,1024]{1,0:T(8,128)(2,1)} async-done(((bf16[128,1024]{1,0:T(8,128)(2,1)}), bf16[1024,1024]{1,0:T(8,128)(2,1)}) %all-gather.3.cloned.1.call-update) | async-done | bytes 2097168 | tf_op jit(solution)/shard_map/all_gather | solution.py:227
  280.8 23.6 %select_reduce_fusion.1 = (f32[1024]{0:T(1024)S(1)}, f32[1024,6288]{0,1:T(8,128)}) fusion(pred[6288]{0:T(1024)(128)(4,1)S(1)} %broadcast_compare_fusion, bf16[1024,1024]{1,0:T(8,128)(2,1)} %all-gather.3.cloned.1.call-done, bf16[6288,1024]{1,0:T(8,128)(2,1)} %param.21), kind=kOutput, calls=%fused_computation.17 | convolution fusion | flops 13199768576 | bytes 40741008 | tf_op jit(solution)/shard_map/dot_general | solution.py:36
  304.5 13.1 %pmax.7 = f32[1024]{0:T(1024)S(1)} all-reduce(f32[1024]{0:T(1024)S(1)} %get-tuple-element.61), channel_id=1, replica_groups=mesh['dp'=4,'vocab'=8] {'vocab'}, use_global_device_ids=true, to_apply=%region_14.16 | all-reduce | flops 1024 | bytes 8192 | tf_op jit(solution)/shard_map/pmax | solution.py:236
  317.6 12.1 %select_reduce_fusion = (f32[1024]{0:T(1024)S(1)}, f32[1024]{0:T(1024)S(1)}, f32[1024]{0:T(1024)S(1)}) fusion(f32[1024,6288]{0,1:T(8,128)} %get-tuple-element.62, pred[6288]{0:T(1024)(128)(4,1)S(1)} %broadcast_compare_fusion, f32[1024]{0:T(1024)S(1)} %pmax.7, s32[1024]{0:T(1024)S(1)} %bitcast.202, s32[6288]{0:T(1024)S(1)} %iota_add_fusion), kind=kLoop, calls=%fused_computation.15 | loop fusion | flops 51508224 | bytes 25807568 | tf_op jit(solution)/shard_map/reduce_sum | solution.py:233
  329.7 22.3 %all-reduce = (f32[1024]{0:T(1024)}, f32[1024]{0:T(1024)}, f32[1024]{0:T(1024)}) all-reduce(f32[1024]{0:T(1024)S(1)} %get-tuple-element.7, f32[1024]{0:T(1024)S(1)} %get-tuple-element.6, f32[1024]{0:T(1024)S(1)} %get-tuple-element.8), channel_id=1, replica_groups=mesh['dp'=4,'vocab'=8] {'vocab'}, use_global_device_ids=true, to_apply=%region_16.18 | all-reduce | flops 3072 | bytes 24576 | tf_op jit(solution)/shard_map/psum | solution.py:238
  353.3 9.5 %all-reduce.1 = (f32[]{:T(128)}, f32[]{:T(128)}) all-reduce(f32[]{:T(128)} %fusion.88, f32[]{:T(128)} %get-tuple-element.21), channel_id=1, replica_groups=mesh['dp'=4,'vocab'=8] {'dp'}, use_global_device_ids=true, to_apply=%region_8.10 | all-reduce | flops 2 | bytes 16 | tf_op jit(solution)/shard_map/psum | solution.py:242
  363.5 28.8 %fusion.6 = f32[1024,1024]{1,0:T(8,128)} fusion(bf16[6288,1024]{1,0:T(8,128)(2,1)} %param.21, f32[1024,6288]{0,1:T(8,128)} %get-tuple-element.62, f32[6288]{0:T(1024)} %broadcast_select_fusion, s32[1024]{0:T(1024)S(1)} %bitcast.203, f32[1024]{0:T(1024)S(1)} %get-tuple-element.22, f32[1024]{0:T(1024)S(1)} %bitcast.212, s32[6288]{0:T(1024)S(1)} %iota_add_fusion, ...), kind=kOutput, calls=%fused_computation.18 | convolution fusion | flops 13238403072 | bytes 42896656 | tf_op jit(solution)/shard_map/dot_general | solution.py:26
  394.4 50.1 %reduce-scatter.5.cloned.1.call-done = f32[128,1024]{1,0:T(8,128)} async-done(((f32[1024,1024]{1,0:T(8,128)}), f32[128,1024]{1,0:T(8,128)}) %reduce-scatter.5.cloned.1.call-update) | async-done | bytes 524304 | tf_op jit(solution)/shard_map/reduce_scatter | solution.py:246
  447.4 6.4 fusion.101
  464.6 5.9 multiply_reduce_fusion
  479.5 3.9 reshape.410
  504.3 127.0 %all-reduce.4.cloned.1.call-done = f32[73728]{0:T(1024)} async-done(((f32[73728]{0:T(1024)}), f32[73728]{0:T(1024)}) %all-reduce.4.cloned.1.call-update) | async-done | bytes 294928 | tf_op jit(solution)/shard_map/psum | solution.py:314
  (309 shorter events, 89.5 us)
Async XLA Ops:
  7.2 83.0 %copy-start = (bf16[1024,1024]{1,0:T(8,128)(2,1)S(1)}, bf16[1024,1024]{1,0:T(8,128)(2,1)}, u32[]{:S(2)}) copy-start(bf16[1024,1024]{1,0:T(8,128)(2,1)} %param.22) | copy-start | bytes 6291460
  7.2 188.2 %reduce-scatter.3.cloned.1.call-start = ((), (), s32[]{:S(2)}) async-start(), calls=%async_computation.2 | async-start | bytes 18874368 | tf_op jit(solution)/shard_map/reduce_scatter | solution.py:135
  79.2 201.7 %all-gather.3.cloned.1.call-start = ((), (), s32[]{:S(2)}) async-start(), calls=%async_computation.3 | async-start | bytes 2359296 | tf_op jit(solution)/shard_map/all_gather | solution.py:227
  81.4 129.7 %copy-start.31 = (bf16[4,1024]{1,0:T(4,128)(2,1)}, bf16[4,1024]{1,0:T(4,128)(2,1)S(1)}, u32[]{:S(2)}) copy-start(bf16[4,1024]{1,0:T(4,128)(2,1)S(1)} %squeeze.21) | copy-start | bytes 24580
  200.7 10.0 %copy-start.5 = (bf16[1024,1024]{1,0:T(8,128)(2,1)}, bf16[1024,1024]{1,0:T(8,128)(2,1)S(1)}, u32[]{:S(2)}) copy-start(bf16[1024,1024]{1,0:T(8,128)(2,1)S(1)} %add_convert_fusion.1) | copy-start | bytes 6291460
  203.3 8.3 %copy-start.29 = (bf16[1024,12]{0,1:T(8,128)(2,1)}, bf16[1024,12]{0,1:T(8,128)(2,1)S(1)}, u32[]{:S(2)}) copy-start(bf16[1024,12]{0,1:T(8,128)(2,1)S(1)} %convolution_convert_fusion.1) | copy-start | bytes 73732
  211.6 19.1 %copy-start.21 = (bf16[128,1024]{0,1:T(8,128)(2,1)}, bf16[128,1024]{0,1:T(8,128)(2,1)S(1)}, u32[]{:S(2)}) copy-start(bf16[128,1024]{0,1:T(8,128)(2,1)S(1)} %copy.45) | copy-start | bytes 786436
  221.8 8.9 %copy-start.7 = (bf16[1024,1024]{0,1:T(8,128)(2,1)}, bf16[1024,1024]{0,1:T(8,128)(2,1)S(1)}, u32[]{:S(2)}) copy-start(bf16[1024,1024]{0,1:T(8,128)(2,1)S(1)} %copy.44) | copy-start | bytes 6291460
  237.0 8.5 %slice-start.2 = ((s8[8388608]{0:T(1024)(128)(4,1)}), s8[4194304]{0:T(1024)(128)(4,1)S(1)}, s32[]{:S(2)}) async-start(s8[8388608]{0:T(1024)(128)(4,1)} %bitcast.163), calls=%async_computation.8 | async-start | bytes 8388608
  251.7 52.8 %copy-start.51 = (f32[128]{0:T(128)}, f32[128]{0:T(128)S(1)}, u32[]{:S(2)}) copy-start(f32[128]{0:T(128)S(1)} %broadcast_multiply_fusion.2) | copy-start | bytes 1540
  251.9 9.8 %copy-start.67 = (f32[128]{0:T(128)}, f32[128]{0:T(128)S(1)}, u32[]{:S(2)}) copy-start(f32[128]{0:T(128)S(1)} %multiply_reduce_fusion.4) | copy-start | bytes 1540
  251.9 9.8 %copy-start.59 = (f32[128]{0:T(128)}, f32[128]{0:T(128)S(1)}, u32[]{:S(2)}) copy-start(f32[128]{0:T(128)S(1)} %fusion.80) | copy-start | bytes 1540
  252.8 191.7 %reduce-scatter.5.cloned.1.call-start = ((), (), s32[]{:S(2)}) async-start(), calls=%async_computation.4 | async-start | bytes 4718592 | tf_op jit(solution)/shard_map/reduce_scatter | solution.py:246
  392.3 52.2 %copy-start.52 = (f32[128]{0:T(128)S(1)}, f32[128]{0:T(128)}, u32[]{:S(2)}) copy-start(f32[128]{0:T(128)} %copy-done.51) | copy-start | bytes 1540
  392.3 53.8 %copy-start.68 = (f32[128]{0:T(128)S(1)}, f32[128]{0:T(128)}, u32[]{:S(2)}) copy-start(f32[128]{0:T(128)} %copy-done.67) | copy-start | bytes 1540
  392.3 53.8 %copy-start.60 = (f32[128]{0:T(128)S(1)}, f32[128]{0:T(128)}, u32[]{:S(2)}) copy-start(f32[128]{0:T(128)} %copy-done.59) | copy-start | bytes 1540
  392.4 238.9 %all-reduce.4.cloned.1.call-start = ((), (), s32[]{:S(2)}) async-start(), calls=%async_computation.5 | async-start | bytes 589824 | tf_op jit(solution)/shard_map/psum | solution.py:314
  447.4 10.5 %slice-start.4 = ((s8[8388608]{0:T(1024)(128)(4,1)}), s8[4194304]{0:T(1024)(128)(4,1)S(1)}, s32[]{:S(2)}) async-start(s8[8388608]{0:T(1024)(128)(4,1)} %bitcast.165), calls=%async_computation.10 | async-start | bytes 8388608
  475.3 10.4 %copy-start.6 = (bf16[16,64,1024]{2,1,0:T(8,128)(2,1)}, bf16[16,64,1024]{2,1,0:T(8,128)(2,1)S(1)}, u32[]{:S(2)}) copy-start(bf16[16,64,1024]{2,1,0:T(8,128)(2,1)S(1)} %multiply_convert_fusion.1) | copy-start | bytes 6291460
  479.5 9.2 %copy-start.36 = (bf16[4,1024]{1,0:T(4,128)(2,1)S(1)}, bf16[4,1024]{1,0:T(4,128)(2,1)}, u32[]{:S(2)}) copy-start(bf16[4,1024]{1,0:T(4,128)(2,1)} %squeeze.25) | copy-start | bytes 24580
  488.7 147.0 %copy-start.1 = (bf16[1024,1024]{1,0:T(8,128)(2,1)S(1)}, bf16[1024,1024]{1,0:T(8,128)(2,1)}, u32[]{:S(2)}) copy-start(bf16[1024,1024]{1,0:T(8,128)(2,1)} %param.22) | copy-start | bytes 6291460
  491.8 141.9 %copy-start.19 = (f32[73728]{0:T(1024)S(1)}, f32[73728]{0:T(1024)}, u32[]{:S(2)}) copy-start(f32[73728]{0:T(1024)} %param.29) | copy-start | bytes 884740
  491.8 141.9 %copy-start.25 = (f32[73728]{0:T(1024)S(1)}, f32[73728]{0:T(1024)}, u32[]{:S(2)}) copy-start(f32[73728]{0:T(1024)} %param.30) | copy-start | bytes 884740
  491.8 141.9 %copy-start.26 = (f32[73728]{0:T(1024)S(1)}, f32[73728]{0:T(1024)}, u32[]{:S(2)}) copy-start(f32[73728]{0:T(1024)} %param.31) | copy-start | bytes 884740
  (62 other events, 231.7 us)
Sparse Core Ops, SparseCore 0:
  79.3 116.0 reduce-scatter.2
  252.9 27.8 all-gather.2
  392.5 51.9 reduce-scatter.4
  503.7 127.4 all-reduce.3
where the time goes:
time: 650 us; the launch traced here: 645 us
  waiting for transfers between devices  292 us (45%)
  matrix products  126 us (19%)
  local copies, waits for them, and re-layouts  98.7 us (15%)
  blocking collectives  63 us (10%)
  other arithmetic  45.7 us (7%)
  between operations  19.6 us (3%)
    psum x1, waiting for transfers between devices, local(): grad_total = lax.psum(local_grad, ('dp', 'vocab'))  127 us
    reduce_scatter x1, waiting for transfers between devices, local(): lax.psum_scatter(jnp.where(inside[:, None], picked.astype(jnp.float32), 0...  96.5 us
    reduce_scatter x1, waiting for transfers between devices, local(): lax.psum_scatter(matrix_multiply(lax.slice_in_dim(grad_logits, 0, rows_he...  50.1 us
    dot_general x17, matrix products, matrix_multiply(): return jnp.dot(left, right, preferred_element_type=jnp.float32)  49.7 us
    gather x1, local copies, waits for them, and re-layouts, local(): jnp.take(shared_embedding, jnp.clip(wanted, 0, shard_rows - 1), axis=0)  47 us
    dot_general x10, matrix products, matrix_multiply_transposed_right(): lax.dot_general(left, right, (((1,), (1,)), ((), ())), preferred_element_...  36.9 us
    psum x1, blocking collectives, local(): lax.psum((local_sum, smooth_local, target_local), 'vocab')  22.3 us
    all_gather x1, waiting for transfers between devices, local(): lax.all_gather(final_rows, 'vocab', axis=0, tiled=True)  17.9 us
  transfers between devices with their start and end apart: 4, of which 4 were waited for; matrix products, arithmetic and copies ran while one was open for 3% of the time, Pallas kernels for 0%

commit v1 on v0

--- a/solution.py
+++ b/solution.py
@@ -311,7 +311,8 @@
         g_bp,
     ]
     local_grad = jnp.concatenate([piece.reshape(-1) for piece in pieces])
-    grad_total = lax.psum(local_grad, ("dp", "vocab"))
+    terms = lax.all_gather(local_grad, ("dp", "vocab"), axis=0, tiled=False)
+    grad_total = terms.sum(axis=0)
     gradient_global_norm = jnp.sqrt(jnp.sum(grad_total * grad_total))
     capped_derivative = grad_total * (GRAD_CLIP / jnp.maximum(gradient_global_norm, GRAD_CLIP))
     refreshed_thin_pairs, updated_first_moment, updated_second_moment = adaptive_moment_update(

time: 650 us -> 608 us (0.935)
  waiting for transfers between devices: 292 us -> 247 us
    psum x1 -> x0, waiting for transfers between devices: 127 us -> none  [local(): grad_total = lax.psum(local_grad, ('dp', 'vocab'))]
    all_gather x0 -> x1, waiting for transfers between devices: none -> 81.5 us  [local(): terms = lax.all_gather(local_grad, ('dp', 'vocab'), axis=0, tiled=False)]
    all_gather x0 -> x1, local copies, waits for them, and re-layouts: none -> 8.24 us  [local(): terms = lax.all_gather(local_grad, ('dp', 'vocab'), axis=0, tiled=False)]
where the time goes in v1:
time: 608 us; the launch traced here: 602 us
  waiting for transfers between devices  247 us (41%)
  matrix products  127 us (21%)
  local copies, waits for them, and re-layouts  97.1 us (16%)
  blocking collectives  63 us (10%)
  other arithmetic  47.8 us (8%)
  between operations  19.9 us (3%)
    reduce_scatter x1, waiting for transfers between devices, local(): lax.psum_scatter(jnp.where(inside[:, None], picked.astype(jnp.float32), 0...  96.5 us
    all_gather x1, waiting for transfers between devices, local(): terms = lax.all_gather(local_grad, ('dp', 'vocab'), axis=0, tiled=False)  81.5 us
    reduce_scatter x1, waiting for transfers between devices, local(): lax.psum_scatter(matrix_multiply(lax.slice_in_dim(grad_logits, 0, rows_he...  50.7 us
    dot_general x17, matrix products, matrix_multiply(): return jnp.dot(left, right, preferred_element_type=jnp.float32)  49.7 us
    gather x1, local copies, waits for them, and re-layouts, local(): jnp.take(shared_embedding, jnp.clip(wanted, 0, shard_rows - 1), axis=0)  47 us
    dot_general x10, matrix products, matrix_multiply_transposed_right(): lax.dot_general(left, right, (((1,), (1,)), ((), ())), preferred_element_...  36.6 us
    psum x1, blocking collectives, local(): lax.psum((local_sum, smooth_local, target_local), 'vocab')  22.3 us
    all_gather x1, waiting for transfers between devices, local(): lax.all_gather(final_rows, 'vocab', axis=0, tiled=True)  17.9 us
  transfers between devices with their start and end apart: 4, of which 4 were waited for; matrix products, arithmetic and copies ran while one was open for 3% of the time, Pallas kernels for 0%

profile of v1, /device:TPU:8, one launch (start us, length us, event | category | flops | bytes accessed | tf_op | source)
XLA Modules:
  0.0 601.5 jit_solution(9102648441063192562)
XLA Ops:
  7.2 9.4 %all-gather.1 = s32[8,1,1024]{2,1,0:T(1,128)S(1)} all-gather(s32[1,1,1024]{2,1,0:T(1,128)} %bitcast.159), channel_id=1, replica_groups=mesh['dp'=4,'vocab'=8] {'vocab'}, dimensions={0}, use_global_device_ids=true | all-gather | bytes 36864 | tf_op jit(solution)/shard_map/all_gather | solution.py:131
  16.9 47.0 %gather_fusion = bf16[8192,1024]{1,0:T(8,128)(2,1)} fusion(bf16[6288,1024]{1,0:T(8,128)(2,1)} %param.21, s32[8192]{0:T(1024)S(1)} %broadcast_clamp_fusion), kind=kCustom, calls=%fused_computation.3 | custom fusion | bytes 33587200 | tf_op jit(solution)/shard_map/jit(_take)/gather | solution.py:134
  63.9 15.2 %select_convert_fusion = bf16[8192,1024]{1,0:T(8,128)(2,1)} fusion(bf16[8192,1024]{1,0:T(8,128)(2,1)} %gather_fusion, pred[8192]{0:T(1024)(128)(4,1)S(1)} %compare_and_fusion.3, pred[8192]{0:T(1024)(128)(4,1)S(1)} %bitcast.197), kind=kLoop, calls=%fused_computation.7 | loop fusion | flops 33554432 | bytes 33570816 | tf_op jit(solution)/shard_map/convert_element_type | solution.py:136
  90.2 5.4 gather_fusion.1
  98.9 96.5 %reduce-scatter.3.cloned.1.call-done = bf16[1024,1024]{1,0:T(8,128)(2,1)} async-done(((bf16[8192,1024]{1,0:T(8,128)(2,1)}), bf16[1024,1024]{1,0:T(8,128)(2,1)}) %reduce-scatter.3.cloned.1.call-update) | async-done | bytes 2097168 | tf_op jit(solution)/shard_map/reduce_scatter | solution.py:135
  203.9 6.8 %fusion.12 = f32[1024,2048]{1,0:T(8,128)} fusion(bf16[1024,1024]{1,0:T(8,128)(2,1)S(1)} %add_convert_fusion.1, bf16[1024,3072]{1,0:T(8,128)(2,1)S(1)} %bitcast.214), kind=kOutput, calls=%fused_computation.34 | convolution fusion | flops 4294967296 | bytes 14680064 | tf_op jit(solution)/shard_map/dot_general | solution.py:26
  211.6 4.8 add_convert_fusion
  221.8 5.0 copy.46
  230.9 6.3 %fusion.98 = (f32[16,128]{1,0:T(8,128)S(1)}, f32[16,128,1024]{2,1,0:T(8,128)}) fusion(pred[128,1024]{1,0:T(8,128)(4,1)} %fusion.62, bf16[128,16,64]{0,2,1:T(8,128)(2,1)S(1)} %bitcast.182, bf16[1024,16,64]{0,2,1:T(8,128)(2,1)S(1)} %bitcast.169), kind=kOutput, calls=%fused_computation.217 | convolution fusion | flops 276825088 | bytes 10887168 | tf_op jit(solution)/shard_map/sub | solution.py:180
  237.8 6.1 %fusion.44 = bf16[16,64,128]{2,1,0:T(8,128)(2,1)S(1)} fusion(bf16[1024,16,64]{0,2,1:T(8,128)(2,1)} %bitcast.180, f32[16,128,1024]{2,1,0:T(8,128)} %get-tuple-element.54, f32[16,128]{1,0:T(8,128)S(1)} %get-tuple-element.53), kind=kOutput, calls=%fused_computation.79 | convolution fusion | flops 272760832 | bytes 10756096 | tf_op jit(solution)/shard_map/hqk,khd->qhd/dot_general | solution.py:184
  253.1 8.8 %all_gather.16 = s32[1024,2]{0,1:T(2,128)S(1)} all-gather(s32[128,2]{0,1:T(2,128)S(1)} %pad_add_fusion), channel_id=1, replica_groups=mesh['dp'=4,'vocab'=8] {'vocab'}, dimensions={0}, use_global_device_ids=true | all-gather | bytes 9216 | tf_op jit(solution)/shard_map/all_gather | solution.py:223
  263.2 17.9 %all-gather.5.cloned.1.call-done = bf16[1024,1024]{1,0:T(8,128)(2,1)} async-done(((bf16[128,1024]{1,0:T(8,128)(2,1)}), bf16[1024,1024]{1,0:T(8,128)(2,1)}) %all-gather.5.cloned.1.call-update) | async-done | bytes 2097168 | tf_op jit(solution)/shard_map/all_gather | solution.py:227
  281.0 23.4 %select_reduce_fusion.1 = (f32[1024]{0:T(1024)S(1)}, f32[1024,6288]{0,1:T(8,128)}) fusion(pred[6288]{0:T(1024)(128)(4,1)S(1)} %broadcast_compare_fusion, bf16[1024,1024]{1,0:T(8,128)(2,1)} %all-gather.5.cloned.1.call-done, bf16[6288,1024]{1,0:T(8,128)(2,1)} %param.21), kind=kOutput, calls=%fused_computation.17 | convolution fusion | flops 13199768576 | bytes 40741008 | tf_op jit(solution)/shard_map/dot_general | solution.py:36
  304.4 13.1 %pmax.7 = f32[1024]{0:T(1024)S(1)} all-reduce(f32[1024]{0:T(1024)S(1)} %get-tuple-element.61), channel_id=1, replica_groups=mesh['dp'=4,'vocab'=8] {'vocab'}, use_global_device_ids=true, to_apply=%region_14.16 | all-reduce | flops 1024 | bytes 8192 | tf_op jit(solution)/shard_map/pmax | solution.py:236
  317.5 12.1 %select_reduce_fusion = (f32[1024]{0:T(1024)S(1)}, f32[1024]{0:T(1024)S(1)}, f32[1024]{0:T(1024)S(1)}) fusion(f32[1024,6288]{0,1:T(8,128)} %get-tuple-element.62, pred[6288]{0:T(1024)(128)(4,1)S(1)} %broadcast_compare_fusion, f32[1024]{0:T(1024)S(1)} %pmax.7, s32[1024]{0:T(1024)S(1)} %bitcast.202, s32[6288]{0:T(1024)S(1)} %iota_add_fusion), kind=kLoop, calls=%fused_computation.15 | loop fusion | flops 51508224 | bytes 25807568 | tf_op jit(solution)/shard_map/reduce_sum | solution.py:233
  329.6 22.3 %all-reduce = (f32[1024]{0:T(1024)}, f32[1024]{0:T(1024)}, f32[1024]{0:T(1024)}) all-reduce(f32[1024]{0:T(1024)S(1)} %get-tuple-element.7, f32[1024]{0:T(1024)S(1)} %get-tuple-element.6, f32[1024]{0:T(1024)S(1)} %get-tuple-element.8), channel_id=1, replica_groups=mesh['dp'=4,'vocab'=8] {'vocab'}, use_global_device_ids=true, to_apply=%region_16.18 | all-reduce | flops 3072 | bytes 24576 | tf_op jit(solution)/shard_map/psum | solution.py:238
  353.3 9.5 %all-reduce.1 = (f32[]{:T(128)}, f32[]{:T(128)}) all-reduce(f32[]{:T(128)} %fusion.88, f32[]{:T(128)} %get-tuple-element.21), channel_id=1, replica_groups=mesh['dp'=4,'vocab'=8] {'dp'}, use_global_device_ids=true, to_apply=%region_8.10 | all-reduce | flops 2 | bytes 16 | tf_op jit(solution)/shard_map/psum | solution.py:242
  363.4 28.9 %fusion.6 = f32[1024,1024]{1,0:T(8,128)} fusion(bf16[6288,1024]{1,0:T(8,128)(2,1)} %param.21, f32[1024,6288]{0,1:T(8,128)} %get-tuple-element.62, f32[6288]{0:T(1024)} %broadcast_select_fusion, s32[1024]{0:T(1024)S(1)} %bitcast.203, f32[1024]{0:T(1024)S(1)} %get-tuple-element.22, f32[1024]{0:T(1024)S(1)} %bitcast.212, s32[6288]{0:T(1024)S(1)} %iota_add_fusion, ...), kind=kOutput, calls=%fused_computation.18 | convolution fusion | flops 13238403072 | bytes 42896656 | tf_op jit(solution)/shard_map/dot_general | solution.py:26
  393.8 50.7 %reduce-scatter.5.cloned.1.call-done = f32[128,1024]{1,0:T(8,128)} async-done(((f32[1024,1024]{1,0:T(8,128)}), f32[128,1024]{1,0:T(8,128)}) %reduce-scatter.5.cloned.1.call-update) | async-done | bytes 524304 | tf_op jit(solution)/shard_map/reduce_scatter | solution.py:246
  447.4 6.4 %fusion.101 = f32[128,4096]{1,0:T(8,128)S(1)} fusion(bf16[128,1024]{1,0:T(8,128)(2,1)S(1)} %add_convert_fusion.5, bf16[4096,1024]{1,0:T(8,128)(2,1)} %param.26), kind=kOutput, calls=%fused_computation.220 | convolution fusion | flops 1073741824 | bytes 10747904 | tf_op jit(solution)/shard_map/dot_general | solution.py:36
  464.6 5.9 multiply_reduce_fusion
  495.3 81.5 %all-gather.7.cloned.1.call-done = f32[2359296]{0:T(1024)} async-done(((f32[73728]{0:T(1024)}), f32[2359296]{0:T(1024)}) %all-gather.7.cloned.1.call-update) | async-done | bytes 9437200 | tf_op jit(solution)/shard_map/all_gather | solution.py:314
  576.9 8.2 %reshape.460 = f32[32,73728]{1,0:T(8,128)} reshape(f32[2359296]{0:T(1024)} %all-gather.7.cloned.1.call-done) | data formatting | bytes 18874368 | tf_op jit(solution)/shard_map/all_gather | solution.py:314
  585.1 4.7 reduce_sum.214
  (311 shorter events, 86.0 us)
Async XLA Ops:
  7.2 83.0 %copy-start = (bf16[1024,1024]{1,0:T(8,128)(2,1)S(1)}, bf16[1024,1024]{1,0:T(8,128)(2,1)}, u32[]{:S(2)}) copy-start(bf16[1024,1024]{1,0:T(8,128)(2,1)} %param.22) | copy-start | bytes 6291460
  7.2 188.2 %reduce-scatter.3.cloned.1.call-start = ((), (), s32[]{:S(2)}) async-start(), calls=%async_computation.2 | async-start | bytes 18874368 | tf_op jit(solution)/shard_map/reduce_scatter | solution.py:135
  79.2 201.9 %all-gather.5.cloned.1.call-start = ((), (), s32[]{:S(2)}) async-start(), calls=%async_computation.3 | async-start | bytes 2359296 | tf_op jit(solution)/shard_map/all_gather | solution.py:227
  81.4 129.7 %copy-start.31 = (bf16[4,1024]{1,0:T(4,128)(2,1)}, bf16[4,1024]{1,0:T(4,128)(2,1)S(1)}, u32[]{:S(2)}) copy-start(bf16[4,1024]{1,0:T(4,128)(2,1)S(1)} %squeeze.21) | copy-start | bytes 24580
  200.7 10.0 %copy-start.5 = (bf16[1024,1024]{1,0:T(8,128)(2,1)}, bf16[1024,1024]{1,0:T(8,128)(2,1)S(1)}, u32[]{:S(2)}) copy-start(bf16[1024,1024]{1,0:T(8,128)(2,1)S(1)} %add_convert_fusion.1) | copy-start | bytes 6291460
  202.7 8.0 %copy-start.20 = (bf16[128,1024]{1,0:T(8,128)(2,1)}, bf16[128,1024]{1,0:T(8,128)(2,1)S(1)}, u32[]{:S(2)}) copy-start(bf16[128,1024]{1,0:T(8,128)(2,1)S(1)} %convolution_convert_fusion) | copy-start | bytes 786436
  203.3 8.3 %copy-start.29 = (bf16[1024,12]{0,1:T(8,128)(2,1)}, bf16[1024,12]{0,1:T(8,128)(2,1)S(1)}, u32[]{:S(2)}) copy-start(bf16[1024,12]{0,1:T(8,128)(2,1)S(1)} %convolution_convert_fusion.1) | copy-start | bytes 73732
  211.6 19.3 %copy-start.21 = (bf16[128,1024]{0,1:T(8,128)(2,1)}, bf16[128,1024]{0,1:T(8,128)(2,1)S(1)}, u32[]{:S(2)}) copy-start(bf16[128,1024]{0,1:T(8,128)(2,1)S(1)} %copy.45) | copy-start | bytes 786436
  221.8 9.1 %copy-start.7 = (bf16[1024,1024]{0,1:T(8,128)(2,1)}, bf16[1024,1024]{0,1:T(8,128)(2,1)S(1)}, u32[]{:S(2)}) copy-start(bf16[1024,1024]{0,1:T(8,128)(2,1)S(1)} %copy.44) | copy-start | bytes 6291460
  237.2 8.5 %slice-start.2 = ((s8[8388608]{0:T(1024)(128)(4,1)}), s8[4194304]{0:T(1024)(128)(4,1)S(1)}, s32[]{:S(2)}) async-start(s8[8388608]{0:T(1024)(128)(4,1)} %bitcast.163), calls=%async_computation.8 | async-start | bytes 8388608
  237.8 7.9 %slice-start.3 = ((s8[8388608]{0:T(1024)(128)(4,1)}), s8[4194304]{0:T(1024)(128)(4,1)S(1)}, s32[]{:S(2)}) async-start(s8[8388608]{0:T(1024)(128)(4,1)} %bitcast.163), calls=%async_computation.9 | async-start | bytes 8388608
  251.9 52.6 %copy-start.51 = (f32[128]{0:T(128)}, f32[128]{0:T(128)S(1)}, u32[]{:S(2)}) copy-start(f32[128]{0:T(128)S(1)} %broadcast_multiply_fusion.2) | copy-start | bytes 1540
  252.1 9.8 %copy-start.67 = (f32[128]{0:T(128)}, f32[128]{0:T(128)S(1)}, u32[]{:S(2)}) copy-start(f32[128]{0:T(128)S(1)} %multiply_reduce_fusion.4) | copy-start | bytes 1540
  252.1 9.8 %copy-start.59 = (f32[128]{0:T(128)}, f32[128]{0:T(128)S(1)}, u32[]{:S(2)}) copy-start(f32[128]{0:T(128)S(1)} %fusion.80) | copy-start | bytes 1540
  253.0 191.5 %reduce-scatter.5.cloned.1.call-start = ((), (), s32[]{:S(2)}) async-start(), calls=%async_computation.4 | async-start | bytes 4718592 | tf_op jit(solution)/shard_map/reduce_scatter | solution.py:246
  392.3 52.2 %copy-start.52 = (f32[128]{0:T(128)S(1)}, f32[128]{0:T(128)}, u32[]{:S(2)}) copy-start(f32[128]{0:T(128)} %copy-done.51) | copy-start | bytes 1540
  392.3 53.8 %copy-start.68 = (f32[128]{0:T(128)S(1)}, f32[128]{0:T(128)}, u32[]{:S(2)}) copy-start(f32[128]{0:T(128)} %copy-done.67) | copy-start | bytes 1540
  392.3 53.8 %copy-start.60 = (f32[128]{0:T(128)S(1)}, f32[128]{0:T(128)}, u32[]{:S(2)}) copy-start(f32[128]{0:T(128)} %copy-done.59) | copy-start | bytes 1540
  392.3 184.5 %all-gather.7.cloned.1.call-start = ((), (), s32[]{:S(2)}) async-start(), calls=%async_computation.5 | async-start | bytes 9732096 | tf_op jit(solution)/shard_map/all_gather | solution.py:314
  447.4 8.2 %copy-start.69 = (f32[128,4096]{1,0:T(8,128)S(1)}, f32[128,4096]{1,0:T(8,128)}, u32[]{:S(2)}) copy-start(f32[128,4096]{1,0:T(8,128)} %get-tuple-element.58) | copy-start | bytes 6291460
  447.4 10.6 %slice-start.4 = ((s8[8388608]{0:T(1024)(128)(4,1)}), s8[4194304]{0:T(1024)(128)(4,1)S(1)}, s32[]{:S(2)}) async-start(s8[8388608]{0:T(1024)(128)(4,1)} %bitcast.165), calls=%async_computation.10 | async-start | bytes 8388608
  478.8 9.7 %copy-start.6 = (bf16[1024,1024]{1,0:T(8,128)(2,1)S(1)}, bf16[1024,1024]{1,0:T(8,128)(2,1)}, u32[]{:S(2)}) copy-start(bf16[1024,1024]{1,0:T(8,128)(2,1)} %copy-done.5) | copy-start | bytes 6291460
  480.2 8.3 %copy-start.36 = (bf16[4,1024]{1,0:T(4,128)(2,1)S(1)}, bf16[4,1024]{1,0:T(4,128)(2,1)}, u32[]{:S(2)}) copy-start(bf16[4,1024]{1,0:T(4,128)(2,1)} %squeeze.25) | copy-start | bytes 24580
  576.9 15.4 %copy-start.1 = (bf16[1024,1024]{1,0:T(8,128)(2,1)S(1)}, bf16[1024,1024]{1,0:T(8,128)(2,1)}, u32[]{:S(2)}) copy-start(bf16[1024,1024]{1,0:T(8,128)(2,1)} %param.22) | copy-start | bytes 6291460
  (62 other events, 222.8 us)
Sparse Core Ops, SparseCore 0:
  79.3 116.0 reduce-scatter.2
  253.1 27.8 all-gather.4
  392.5 51.9 reduce-scatter.4
  494.8 82.0 all-gather.6
